TPU v7x, 32 devices: a whole 2x2x4 slice. The times are simulated.
32 devices in a mesh: tiles: 8 (over z, x), lev: 4 (over y, core).
Axes of the slice: x: 2, y: 2, z: 4, core: 2. Of those that a mesh axis runs over, the one named last changes fastest.
Arguments:
- land_smb: bfloat16 [512, 10, 128], P(('tiles', 'lev')), may hold values from -6 to 6
- block_weights: bfloat16 [1024, 128, 1024], P(('tiles', 'lev')), may hold values from -0.5 to 0.5
- block_tile: int32 [1024], P(('tiles', 'lev')), may hold values from 0 to 255, as said below
- block_land: int32 [1024], P(('tiles', 'lev')), may hold values from 0 to 15
- block_class: int32 [1024], P(('tiles', 'lev')), may hold values from 0 to 9
- ice_mask: int32 [64, 4096], P('tiles', 'lev'), may hold values 0 or 1
- thickness: float32 [64, 4096], P('tiles', 'lev'), may hold values from 0.5 to 2
- prev_smb: float32 [64, 4096], P('tiles', 'lev'), may hold values from -6 to 6
- basal_friction: float32 [64, 4096], P('tiles', 'lev'), may hold values from 0.05 to 0.5
- driving: float32 [10, 64, 4096], P(None, 'tiles', 'lev'), may hold values from -54 to 54
- velocity_start: float32 [10, 64, 4096], P(None, 'tiles', 'lev'), may hold values from -6 to 6
Outputs:
- ice_smb: float32 [64, 4096], P('tiles')
- velocity_end: float32 [10, 64, 4096], P(None, 'tiles', 'lev')
Inputs may be any that keep to these rules, and one draw needn't show every extreme that they name: `block_tile`: ice tile t lies on index t // 32 of tiles. Of the 32 remap blocks of one device, at most 8 name tiles on any one index of tiles; in every draw some index of tiles receives exactly 8 from every device.
All inputs are finite; a program needn't handle non-finite values. No bound on the sum of `ice_mask` on one device may be relied on, other than what follows from the above.
Results may differ from a plain program's by a relative error of at most 0.0003.
Values sent between devices are 32-bit elements; how exact they have to be, the bound alone decides.
A program may use at most 64 MiB of HBM per device.

v0:
```python
import jax
import jax.numpy as jnp
from jax import lax
from jax.sharding import PartitionSpec as P

CX = 8
TW = 128
TPD = 32
ITERS = 4
VISC_FLOOR = 0.25
VERTICAL = 4.0
SMB_WEIGHT = 0.5


def extended(cells, sides, width):
    for axis, dim in sides:
        count = lax.axis_size(axis)
        ends = count - 1
        head = lax.slice_in_dim(cells, 0, width, axis=dim)
        tail = lax.slice_in_dim(cells, cells.shape[dim] - width, cells.shape[dim], axis=dim)
        cells = jnp.concatenate(
            [
                lax.ppermute(tail, axis, [(i, (i + 1) % count) for i in range(ends)]),
                cells,
                lax.ppermute(head, axis, [((i + 1) % count, i) for i in range(ends)]),
            ],
            axis=dim,
        )
    return cells


def visc_from(box, ice_frac):
    slope_x = (box[:, 2:, 1:-1] - box[:, :-2, 1:-1]) * 0.5
    slope_y = (box[:, 1:-1, 2:] - box[:, 1:-1, :-2]) * 0.5
    return ice_frac * (VISC_FLOOR + slope_x * slope_x + slope_y * slope_y) ** (-1.0 / 3.0)


def level_pad(box):
    return jnp.pad(box, ((1, 1), (0, 0), (0, 0)))


def face_weights(visc_box, drag):
    center = visc_box[1:-1, 1:-1, 1:-1]
    east_face = jnp.sqrt(center * visc_box[1:-1, 2:, 1:-1])
    west_face = jnp.sqrt(center * visc_box[1:-1, :-2, 1:-1])
    north_face = jnp.sqrt(center * visc_box[1:-1, 1:-1, 2:])
    south_face = jnp.sqrt(center * visc_box[1:-1, 1:-1, :-2])
    upper_face = VERTICAL * jnp.sqrt(center * visc_box[2:, 1:-1, 1:-1])
    lower_face = VERTICAL * jnp.sqrt(center * visc_box[:-2, 1:-1, 1:-1])
    diagonal_sum = drag + east_face + west_face + north_face + south_face + upper_face + lower_face
    return (diagonal_sum, east_face, west_face, upper_face, lower_face, north_face, south_face)


def apply_operator(faces, field_box):
    diagonal_sum, east_face, west_face, upper_face, lower_face, north_face, south_face = faces
    center = field_box[1:-1, 1:-1, 1:-1]
    result = (
        diagonal_sum * center
        - east_face * field_box[1:-1, 2:, 1:-1]
        - west_face * field_box[1:-1, :-2, 1:-1]
    )
    result = (
        result - upper_face * field_box[2:, 1:-1, 1:-1] - lower_face * field_box[:-2, 1:-1, 1:-1]
    )
    return result - north_face * field_box[1:-1, 1:-1, 2:] - south_face * field_box[1:-1, 1:-1, :-2]


def apply_local(faces, field):
    field_box = extended(field, (("tiles", 1), ("lev", 2)), 1)
    return apply_operator(faces, level_pad(field_box))


def paired_totals(residual, image):
    return lax.psum((jnp.sum(residual * residual), jnp.sum(residual * image)), ("tiles", "lev"))


def krylov_merged(faces, rhs, start):
    solution = start
    residual = rhs - apply_local(faces, start)
    image = apply_local(faces, residual)
    norm_now, product = paired_totals(residual, image)
    step_len = norm_now / product
    direction = residual
    along = image
    for iteration in range(ITERS):
        solution = solution + step_len * direction
        residual = residual - step_len * along
        if iteration + 1 < ITERS:
            image = apply_local(faces, residual)
            norm_next, product = paired_totals(residual, image)
            ratio = norm_next / norm_now
            step_len = norm_next / (product - ratio * norm_next / step_len)
            direction = residual + ratio * direction
            along = image + ratio * along
            norm_now = norm_next
    return solution


def sent_visc(velocity, ice_frac):
    x_box = extended(velocity, (("tiles", 1), ("lev", 2)), 1)
    viscosity = visc_from(x_box, ice_frac)
    visc_box = extended(viscosity, (("tiles", 1), ("lev", 2)), 1)
    return level_pad(visc_box)


def body(
    land_smb,
    block_weights,
    block_tile,
    block_land,
    block_class,
    ice_mask,
    thickness,
    prev_smb,
    basal_friction,
    driving,
    velocity_start,
):
    local_blocks, classes, land_cols = land_smb.shape
    blocks_here = block_tile.shape[0]
    tile_cells = block_weights.shape[2]
    land_rows = land_smb.reshape(local_blocks * classes, land_cols)
    picked = land_rows[block_land * classes + block_class]
    products = jnp.einsum("bl,blt->bt", picked, block_weights, preferred_element_type=jnp.float32)
    owners = lax.axis_size("tiles")
    capacity = max(2, 2 * blocks_here // owners)
    destination = block_tile // TPD
    local_tile = block_tile % TPD
    positions = jnp.arange(blocks_here, dtype=jnp.int32)
    earlier = jnp.logical_and(
        destination[None, :] == destination[:, None], positions[None, :] < positions[:, None]
    )
    ranks = jnp.sum(earlier.astype(jnp.int32), axis=1)
    slots = destination * capacity + ranks
    slot_ids = jnp.arange(owners * capacity, dtype=jnp.int32)
    slot_match = slots[None, :] == slot_ids[:, None]
    slot_hot = slot_match.astype(jnp.float32)
    sending = jnp.dot(
        slot_hot, products, precision=lax.Precision.HIGHEST, preferred_element_type=jnp.float32
    )
    sending = sending.reshape(owners, capacity, tile_cells)
    slot_tile = jnp.sum(jnp.where(slot_match, (local_tile + 1)[None, :], 0), axis=1) - 1
    slot_tile = slot_tile.reshape(owners, capacity)
    received, recv_tile = (
        lax.all_to_all(sending, "tiles", split_axis=0, concat_axis=0, tiled=True),
        lax.all_to_all(slot_tile, "tiles", split_axis=0, concat_axis=0, tiled=True),
    )
    tile_hot = (recv_tile.reshape(-1)[None, :] == jnp.arange(TPD, dtype=jnp.int32)[:, None]).astype(
        jnp.float32
    )
    partial_sums = jnp.dot(
        tile_hot,
        received.reshape(-1, tile_cells),
        precision=lax.Precision.HIGHEST,
        preferred_element_type=jnp.float32,
    )
    totals = lax.psum(partial_sums, "lev")
    ice_smb = totals.reshape(TPD, CX, TW).transpose(1, 0, 2).reshape(CX, TPD * TW)
    ice_frac = ice_mask.astype(jnp.float32)
    rhs = (ice_frac * (thickness + SMB_WEIGHT * prev_smb))[None] * driving
    drag = (ice_frac * basal_friction + (1.0 - ice_frac))[None]
    velocity = velocity_start
    visc_box = sent_visc(velocity, ice_frac[None])
    faces = face_weights(visc_box, drag)
    velocity = krylov_merged(faces, rhs, velocity)
    return (ice_smb, velocity)


def solution(mesh):
    in_specs = (
        P(("tiles", "lev"), None, None),
        P(("tiles", "lev"), None, None),
        P(("tiles", "lev")),
        P(("tiles", "lev")),
        P(("tiles", "lev")),
        P("tiles", "lev"),
        P("tiles", "lev"),
        P("tiles", "lev"),
        P("tiles", "lev"),
        P(None, "tiles", "lev"),
        P(None, "tiles", "lev"),
    )
    out_specs = (P("tiles", None), P(None, "tiles", "lev"))
    return jax.shard_map(body, mesh=mesh, in_specs=in_specs, out_specs=out_specs, check_vma=False)
```

profile of v0, /device:TPU:0, one launch (start us, length us, event | category | flops | bytes accessed | tf_op | source)
XLA Modules:
  0.0 379.7 jit_solution(6685467221838924000)
XLA Ops:
  8.3 1.3 collective-permute-start
  9.6 5.5 %collective-permute-start.1 = (f32[10,1,1024]{2,1,0:T(1,128)S(1)}, f32[10,1,1024]{2,1,0:T(1,128)S(1)}, u32[]{:S(2)}, u32[]{:S(2)}) collective-permute-start(f32[10,1,1024]{2,1,0:T(1,128)S(1)} %get-tuple-element.46), channel_id=1, source_target_pairs={{0,4},{4,8},{8,12},{12,16},{16,20},{20,24},{24,28},{1,5},{5,9},{9,... | collective-permute-start | bytes 122888 | tf_op jit(solution)/shard_map/ppermute | solution.py:23
  15.2 1.6 collective-permute-done.1
  18.0 1.3 collective-permute-start.2
  19.3 3.0 collective-permute-start.3
  22.3 1.4 add_multiply_fusion
  24.5 2.2 power_multiply_fusion
  26.8 1.3 collective-permute-start.4
  28.1 5.4 %collective-permute-start.5 = (f32[10,1,1024]{2,1,0:T(1,128)S(1)}, f32[10,1,1024]{2,1,0:T(1,128)S(1)}, u32[]{:S(2)}, u32[]{:S(2)}) collective-permute-start(f32[10,1,1024]{2,1,0:T(1,128)S(1)} %get-tuple-element.44), channel_id=1, source_target_pairs={{0,4},{4,8},{8,12},{12,16},{16,20},{20,24},{24,28},{1,5},{5,9},{9,... | collective-permute-start | bytes 122888 | tf_op jit(solution)/shard_map/ppermute | solution.py:23
  35.9 1.3 collective-permute-start.6
  37.2 3.0 collective-permute-start.7
  42.0 3.4 fusion.11
  45.5 1.3 collective-permute-start.8
  46.8 5.4 %collective-permute-start.9 = (f32[10,1,1024]{2,1,0:T(1,128)S(1)}, f32[10,1,1024]{2,1,0:T(1,128)S(1)}, u32[]{:S(2)}, u32[]{:S(2)}) collective-permute-start(f32[10,1,1024]{2,1,0:T(1,128)S(1)} %get-tuple-element.42), channel_id=1, source_target_pairs={{0,4},{4,8},{8,12},{12,16},{16,20},{20,24},{24,28},{1,5},{5,9},{9,... | collective-permute-start | bytes 122888 | tf_op jit(solution)/shard_map/ppermute | solution.py:23
  54.1 3.5 collective-permute-start.10
  57.6 1.3 collective-permute-start.11
  59.6 3.9 %collective-permute-done.11 = f32[10,10,1]{2,1,0:T(8,128)S(1)} collective-permute-done((f32[10,10,1]{2,1,0:T(8,128)S(1)}, f32[10,10,1]{2,1,0:T(8,128)S(1)}, u32[]{:S(2)}, u32[]{:S(2)}) %collective-permute-start.11) | collective-permute-done | bytes 432 | tf_op jit(solution)/shard_map/ppermute | solution.py:25
  64.6 3.3 multiply_reduce_fusion.5
  67.9 45.4 %all-reduce.9 = (f32[]{:T(128)}, f32[]{:T(128)}) all-reduce(f32[]{:T(128)} %get-tuple-element.7, f32[]{:T(128)} %get-tuple-element.6), channel_id=1, replica_groups=mesh['tiles'=8,'lev'=4] {'tiles','lev'}, use_global_device_ids=true, to_apply=%region_4.5 | all-reduce | flops 2 | bytes 16 | tf_op jit(solution)/shard_map/psum | solution.py:74
  114.6 1.3 collective-permute-start.12
  115.9 4.8 %collective-permute-start.13 = (f32[10,1,1024]{2,1,0:T(1,128)S(1)}, f32[10,1,1024]{2,1,0:T(1,128)S(1)}, u32[]{:S(2)}, u32[]{:S(2)}) collective-permute-start(f32[10,1,1024]{2,1,0:T(1,128)S(1)} %get-tuple-element.40), channel_id=1, source_target_pairs={{0,4},{4,8},{8,12},{12,16},{16,20},{20,24},{24,28},{1,5},{5,9},{9,... | collective-permute-start | bytes 122888 | tf_op jit(solution)/shard_map/ppermute | solution.py:23
  121.4 5.9 %all-to-all-start = ((s32[8,1,8]{2,1,0:T(1,128)}), s32[8,1,8]{2,1,0:T(1,128)}, u32[]{:S(2)}, u32[]{:S(2)}) async-start(s32[8,1,8]{2,1,0:T(1,128)} %bitcast), calls=%async_computation | async-start | bytes 8192 | tf_op jit(solution)/shard_map/all_to_all | solution.py:146
  127.6 1.3 collective-permute-start.14
  128.9 1.3 collective-permute-start.15
  131.4 3.0 collective-permute-done.15
  135.6 3.3 multiply_reduce_fusion.3
  138.8 42.6 %all-reduce.8 = (f32[]{:T(128)}, f32[]{:T(128)}) all-reduce(f32[]{:T(128)} %get-tuple-element.5, f32[]{:T(128)} %get-tuple-element.4), channel_id=1, replica_groups=mesh['tiles'=8,'lev'=4] {'tiles','lev'}, use_global_device_ids=true, to_apply=%region_8.9 | all-reduce | flops 2 | bytes 16 | tf_op jit(solution)/shard_map/psum | solution.py:74
  186.2 1.3 collective-permute-start.16
  187.5 4.8 %collective-permute-start.17 = (f32[10,1,1024]{2,1,0:T(1,128)S(1)}, f32[10,1,1024]{2,1,0:T(1,128)S(1)}, u32[]{:S(2)}, u32[]{:S(2)}) collective-permute-start(f32[10,1,1024]{2,1,0:T(1,128)S(1)} %get-tuple-element.38), channel_id=1, source_target_pairs={{0,4},{4,8},{8,12},{12,16},{16,20},{20,24},{24,28},{1,5},{5,9},{9,... | collective-permute-start | bytes 122888 | tf_op jit(solution)/shard_map/ppermute | solution.py:23
  196.5 1.3 collective-permute-start.18
  197.8 1.5 collective-permute-start.19
  199.2 5.2 %fusion.74 = f32[32,1,1024]{2,1,0:T(1,128)} fusion(bf16[32,128,1024]{2,1,0:T(8,128)(2,1)} %param.12, bf16[32,128,1]{1,0,2:T(8,128)(2,1)S(1)} %bitcast.19), kind=kOutput, calls=%fused_computation.159 | convolution fusion | flops 8388608 | bytes 8527872 | tf_op jit(solution)/shard_map/bl,blt->bt/dot_general | solution.py:124
  204.5 2.3 concatenate.141
  206.8 4.0 %multiply_reduce_fusion.1 = (f32[]{:T(128)}, f32[]{:T(128)}, f32[10,8,1024]{2,1,0:T(8,128)}) fusion(f32[10,8,1024]{2,1,0:T(8,128)S(1)} %multiply_subtract_fusion.1, f32[10,1,1024]{2,1,0:T(1,128)S(1)} %collective-permute-done.16, f32[10,1,1024]{2,1,0:T(1,128)S(1)} %collective-permute-done.17, f32[10,10,1]{2,1,0:T(8,128)S(1)} %collective-permute-done.18, ...), kind=kLoop, calls=%fused_computation.142 | loop fusion | flops 3522558 | bytes 2247016 | tf_op jit(solution)/shard_map/reduce_sum | solution.py:74
  210.8 44.5 %all-reduce.7 = (f32[]{:T(128)}, f32[]{:T(128)}) all-reduce(f32[]{:T(128)} %get-tuple-element.3, f32[]{:T(128)} %get-tuple-element.2), channel_id=1, replica_groups=mesh['tiles'=8,'lev'=4] {'tiles','lev'}, use_global_device_ids=true, to_apply=%region_12.13 | all-reduce | flops 2 | bytes 16 | tf_op jit(solution)/shard_map/psum | solution.py:74
  259.1 1.8 multiply_reduce_fusion
  260.9 1.3 collective-permute-start.20
  262.2 4.8 %collective-permute-start.21 = (f32[10,1,1024]{2,1,0:T(1,128)S(1)}, f32[10,1,1024]{2,1,0:T(1,128)S(1)}, u32[]{:S(2)}, u32[]{:S(2)}) collective-permute-start(f32[10,1,1024]{2,1,0:T(1,128)S(1)} %get-tuple-element.36), channel_id=1, source_target_pairs={{0,4},{4,8},{8,12},{12,16},{16,20},{20,24},{24,28},{1,5},{5,9},{9,... | collective-permute-start | bytes 122888 | tf_op jit(solution)/shard_map/ppermute | solution.py:23
  267.0 2.0 convolution_bitcast_fusion
  270.3 6.3 %all-to-all-start.1 = ((f32[8,8,1024]{2,1,0:T(8,128)}), f32[8,8,1024]{2,1,0:T(8,128)}, u32[]{:S(2)}, u32[]{:S(2)}) async-start(f32[8,8,1024]{2,1,0:T(8,128)} %convolution_bitcast_fusion), calls=%async_computation.1 | async-start | bytes 524288 | tf_op jit(solution)/shard_map/all_to_all | solution.py:145
  277.4 1.9 collective-permute-start.22
  281.1 1.9 reduce.3
  283.0 1.3 eq.49
  284.7 2.1 concatenate.147
  286.8 3.4 fusion.70
  290.2 43.7 %all-reduce.6 = (f32[]{:T(128)}, f32[]{:T(128)}) all-reduce(f32[]{:T(128)} %get-tuple-element.16, f32[]{:T(128)} %fusion.70), channel_id=1, replica_groups=mesh['tiles'=8,'lev'=4] {'tiles','lev'}, use_global_device_ids=true, to_apply=%region_16.17 | all-reduce | flops 2 | bytes 16 | tf_op jit(solution)/shard_map/psum | solution.py:74
  340.2 31.1 %all-reduce.12.cloned.1.call-done = f32[8,4096]{1,0:T(8,128)} async-done(((f32[8,4096]{1,0:T(8,128)}), f32[8,4096]{1,0:T(8,128)}) %all-reduce.12.cloned.1.call-update) | async-done | bytes 131088 | tf_op jit(solution)/shard_map/psum | solution.py:157
  371.3 1.6 copy.29
  (96 shorter events, 25.6 us)
Async XLA Ops:
  8.3 6.8 %collective-permute-start = (f32[10,1,1024]{2,1,0:T(1,128)S(1)}, f32[10,1,1024]{2,1,0:T(1,128)S(1)}, u32[]{:S(2)}, u32[]{:S(2)}) collective-permute-start(f32[10,1,1024]{2,1,0:T(1,128)S(1)} %get-tuple-element.47), channel_id=1, source_target_pairs={{4,0},{8,4},{12,8},{16,12},{20,16},{24,20},{28,24},{5,1},{9,5},{13... | collective-permute-start | bytes 122888 | tf_op jit(solution)/shard_map/ppermute | solution.py:25
  9.6 7.2 %collective-permute-start.1 = (f32[10,1,1024]{2,1,0:T(1,128)S(1)}, f32[10,1,1024]{2,1,0:T(1,128)S(1)}, u32[]{:S(2)}, u32[]{:S(2)}) collective-permute-start(f32[10,1,1024]{2,1,0:T(1,128)S(1)} %get-tuple-element.46), channel_id=1, source_target_pairs={{0,4},{4,8},{8,12},{12,16},{16,20},{20,24},{24,28},{1,5},{5,9},{9,... | collective-permute-start | bytes 122888 | tf_op jit(solution)/shard_map/ppermute | solution.py:23
  15.1 19.6 %copy-start.9 = (f32[10,1,1024]{2,1,0:T(1,128)}, f32[10,1,1024]{2,1,0:T(1,128)S(1)}, u32[]{:S(2)}) copy-start(f32[10,1,1024]{2,1,0:T(1,128)S(1)} %collective-permute-done) | copy-start | bytes 122884
  16.8 18.0 %copy-start.10 = (f32[10,1,1024]{2,1,0:T(1,128)}, f32[10,1,1024]{2,1,0:T(1,128)S(1)}, u32[]{:S(2)}) copy-start(f32[10,1,1024]{2,1,0:T(1,128)S(1)} %collective-permute-done.1) | copy-start | bytes 122884
  18.0 6.5 %collective-permute-start.2 = (f32[10,10,1]{2,1,0:T(8,128)S(1)}, f32[10,10,1]{2,1,0:T(8,128)S(1)}, u32[]{:S(2)}, u32[]{:S(2)}) collective-permute-start(f32[10,10,1]{2,1,0:T(8,128)S(1)} %get-tuple-element.34), channel_id=1, source_target_pairs={{1,0},{2,1},{3,2},{5,4},{6,5},{7,6},{9,8},{10,9},{11,10},{13,12},{... | collective-permute-start | bytes 1208 | tf_op jit(solution)/shard_map/ppermute | solution.py:25
  19.3 5.2 %collective-permute-start.3 = (f32[10,10,1]{2,1,0:T(8,128)S(1)}, f32[10,10,1]{2,1,0:T(8,128)S(1)}, u32[]{:S(2)}, u32[]{:S(2)}) collective-permute-start(f32[10,10,1]{2,1,0:T(8,128)S(1)} %get-tuple-element.35), channel_id=1, source_target_pairs={{0,1},{1,2},{2,3},{4,5},{5,6},{6,7},{8,9},{9,10},{10,11},{12,13},{... | collective-permute-start | bytes 1208 | tf_op jit(solution)/shard_map/ppermute | solution.py:23
  24.5 17.3 %copy-start.7 = (f32[10,10,1]{2,1,0:T(8,128)}, f32[10,10,1]{2,1,0:T(8,128)S(1)}, u32[]{:S(2)}) copy-start(f32[10,10,1]{2,1,0:T(8,128)S(1)} %collective-permute-done.2) | copy-start | bytes 1204
  24.5 17.3 %copy-start.8 = (f32[10,10,1]{2,1,0:T(8,128)}, f32[10,10,1]{2,1,0:T(8,128)S(1)}, u32[]{:S(2)}) copy-start(f32[10,10,1]{2,1,0:T(8,128)S(1)} %collective-permute-done.3) | copy-start | bytes 1204
  26.8 7.9 %collective-permute-start.4 = (f32[10,1,1024]{2,1,0:T(1,128)S(1)}, f32[10,1,1024]{2,1,0:T(1,128)S(1)}, u32[]{:S(2)}, u32[]{:S(2)}) collective-permute-start(f32[10,1,1024]{2,1,0:T(1,128)S(1)} %get-tuple-element.45), channel_id=1, source_target_pairs={{4,0},{8,4},{12,8},{16,12},{20,16},{24,20},{28,24},{5,1},{9,5},{13... | collective-permute-start | bytes 122888 | tf_op jit(solution)/shard_map/ppermute | solution.py:25
  28.1 7.6 %collective-permute-start.5 = (f32[10,1,1024]{2,1,0:T(1,128)S(1)}, f32[10,1,1024]{2,1,0:T(1,128)S(1)}, u32[]{:S(2)}, u32[]{:S(2)}) collective-permute-start(f32[10,1,1024]{2,1,0:T(1,128)S(1)} %get-tuple-element.44), channel_id=1, source_target_pairs={{0,4},{4,8},{8,12},{12,16},{16,20},{20,24},{24,28},{1,5},{5,9},{9,... | collective-permute-start | bytes 122888 | tf_op jit(solution)/shard_map/ppermute | solution.py:23
  34.7 6.6 %copy-start.14 = (s32[32]{0:T(128)}, s32[32]{0:T(128)S(1)}, u32[]{:S(2)}) copy-start(s32[32]{0:T(128)S(1)} %get-tuple-element.51) | copy-start | bytes 388
  34.7 5.5 %copy-start.3 = (f32[10,1,1024]{2,1,0:T(1,128)}, f32[10,1,1024]{2,1,0:T(1,128)S(1)}, u32[]{:S(2)}) copy-start(f32[10,1,1024]{2,1,0:T(1,128)S(1)} %collective-permute-done.4) | copy-start | bytes 122884
  35.6 4.6 %copy-start.5 = (f32[10,1,1024]{2,1,0:T(1,128)}, f32[10,1,1024]{2,1,0:T(1,128)S(1)}, u32[]{:S(2)}) copy-start(f32[10,1,1024]{2,1,0:T(1,128)S(1)} %collective-permute-done.5) | copy-start | bytes 122884
  35.9 5.5 %collective-permute-start.6 = (f32[10,10,1]{2,1,0:T(8,128)S(1)}, f32[10,10,1]{2,1,0:T(8,128)S(1)}, u32[]{:S(2)}, u32[]{:S(2)}) collective-permute-start(f32[10,10,1]{2,1,0:T(8,128)S(1)} %get-tuple-element.33), channel_id=1, source_target_pairs={{1,0},{2,1},{3,2},{5,4},{6,5},{7,6},{9,8},{10,9},{11,10},{13,12},{... | collective-permute-start | bytes 1208 | tf_op jit(solution)/shard_map/ppermute | solution.py:25
  37.2 4.2 %collective-permute-start.7 = (f32[10,10,1]{2,1,0:T(8,128)S(1)}, f32[10,10,1]{2,1,0:T(8,128)S(1)}, u32[]{:S(2)}, u32[]{:S(2)}) collective-permute-start(f32[10,10,1]{2,1,0:T(8,128)S(1)} %get-tuple-element.32), channel_id=1, source_target_pairs={{0,1},{1,2},{2,3},{4,5},{5,6},{6,7},{8,9},{9,10},{10,11},{12,13},{... | collective-permute-start | bytes 1208 | tf_op jit(solution)/shard_map/ppermute | solution.py:23
  41.4 0.6 copy-start.1
  45.4 90.2 %copy-start.2 = (f32[10,10,1]{2,1,0:T(8,128)S(1)}, f32[10,10,1]{2,1,0:T(8,128)}, u32[]{:S(2)}) copy-start(f32[10,10,1]{2,1,0:T(8,128)} %copy-done.1) | copy-start | bytes 1204
  45.4 90.2 %copy-start.4 = (f32[10,1,1024]{2,1,0:T(1,128)S(1)}, f32[10,1,1024]{2,1,0:T(1,128)}, u32[]{:S(2)}) copy-start(f32[10,1,1024]{2,1,0:T(1,128)} %copy-done.3) | copy-start | bytes 122884
  45.4 90.2 %copy-start.6 = (f32[10,1,1024]{2,1,0:T(1,128)S(1)}, f32[10,1,1024]{2,1,0:T(1,128)}, u32[]{:S(2)}) copy-start(f32[10,1,1024]{2,1,0:T(1,128)} %copy-done.5) | copy-start | bytes 122884
  45.5 7.4 %collective-permute-start.8 = (f32[10,1,1024]{2,1,0:T(1,128)S(1)}, f32[10,1,1024]{2,1,0:T(1,128)S(1)}, u32[]{:S(2)}, u32[]{:S(2)}) collective-permute-start(f32[10,1,1024]{2,1,0:T(1,128)S(1)} %get-tuple-element.43), channel_id=1, source_target_pairs={{4,0},{8,4},{12,8},{16,12},{20,16},{24,20},{28,24},{5,1},{9,5},{13... | collective-permute-start | bytes 122888 | tf_op jit(solution)/shard_map/ppermute | solution.py:25
  46.8 7.1 %collective-permute-start.9 = (f32[10,1,1024]{2,1,0:T(1,128)S(1)}, f32[10,1,1024]{2,1,0:T(1,128)S(1)}, u32[]{:S(2)}, u32[]{:S(2)}) collective-permute-start(f32[10,1,1024]{2,1,0:T(1,128)S(1)} %get-tuple-element.42), channel_id=1, source_target_pairs={{0,4},{4,8},{8,12},{12,16},{16,20},{20,24},{24,28},{1,5},{5,9},{9,... | collective-permute-start | bytes 122888 | tf_op jit(solution)/shard_map/ppermute | solution.py:23
  52.9 74.5 %copy-start.13 = (s32[32]{0:T(128)}, s32[32]{0:T(128)S(1)}, u32[]{:S(2)}) copy-start(s32[32]{0:T(128)S(1)} %multiply_add_fusion.2) | copy-start | bytes 388
  54.1 5.5 %collective-permute-start.10 = (f32[10,10,1]{2,1,0:T(8,128)S(1)}, f32[10,10,1]{2,1,0:T(8,128)S(1)}, u32[]{:S(2)}, u32[]{:S(2)}) collective-permute-start(f32[10,10,1]{2,1,0:T(8,128)S(1)} %get-tuple-element.31), channel_id=1, source_target_pairs={{0,1},{1,2},{2,3},{4,5},{5,6},{6,7},{8,9},{9,10},{10,11},{12,13},{... | collective-permute-start | bytes 1208 | tf_op jit(solution)/shard_map/ppermute | solution.py:23
  57.6 5.9 %collective-permute-start.11 = (f32[10,10,1]{2,1,0:T(8,128)S(1)}, f32[10,10,1]{2,1,0:T(8,128)S(1)}, u32[]{:S(2)}, u32[]{:S(2)}) collective-permute-start(f32[10,10,1]{2,1,0:T(8,128)S(1)} %get-tuple-element.30), channel_id=1, source_target_pairs={{1,0},{2,1},{3,2},{5,4},{6,5},{7,6},{9,8},{10,9},{11,10},{13,12},{... | collective-permute-start | bytes 1208 | tf_op jit(solution)/shard_map/ppermute | solution.py:25
  114.6 12.7 %collective-permute-start.12 = (f32[10,1,1024]{2,1,0:T(1,128)S(1)}, f32[10,1,1024]{2,1,0:T(1,128)S(1)}, u32[]{:S(2)}, u32[]{:S(2)}) collective-permute-start(f32[10,1,1024]{2,1,0:T(1,128)S(1)} %get-tuple-element.41), channel_id=1, source_target_pairs={{4,0},{8,4},{12,8},{16,12},{20,16},{24,20},{28,24},{5,1},{9,5},{13... | collective-permute-start | bytes 122888 | tf_op jit(solution)/shard_map/ppermute | solution.py:25
  115.9 11.4 %collective-permute-start.13 = (f32[10,1,1024]{2,1,0:T(1,128)S(1)}, f32[10,1,1024]{2,1,0:T(1,128)S(1)}, u32[]{:S(2)}, u32[]{:S(2)}) collective-permute-start(f32[10,1,1024]{2,1,0:T(1,128)S(1)} %get-tuple-element.40), channel_id=1, source_target_pairs={{0,4},{4,8},{8,12},{12,16},{16,20},{20,24},{24,28},{1,5},{5,9},{9,... | collective-permute-start | bytes 122888 | tf_op jit(solution)/shard_map/ppermute | solution.py:23
  121.4 148.9 %all-to-all-start = ((s32[8,1,8]{2,1,0:T(1,128)}), s32[8,1,8]{2,1,0:T(1,128)}, u32[]{:S(2)}, u32[]{:S(2)}) async-start(s32[8,1,8]{2,1,0:T(1,128)} %bitcast), calls=%async_computation | async-start | bytes 8192 | tf_op jit(solution)/shard_map/all_to_all | solution.py:146
  127.6 3.8 collective-permute-start.14
  128.9 5.5 %collective-permute-start.15 = (f32[10,10,1]{2,1,0:T(8,128)S(1)}, f32[10,10,1]{2,1,0:T(8,128)S(1)}, u32[]{:S(2)}, u32[]{:S(2)}) collective-permute-start(f32[10,10,1]{2,1,0:T(8,128)S(1)} %get-tuple-element.28), channel_id=1, source_target_pairs={{1,0},{2,1},{3,2},{5,4},{6,5},{7,6},{9,8},{10,9},{11,10},{13,12},{... | collective-permute-start | bytes 1208 | tf_op jit(solution)/shard_map/ppermute | solution.py:25
  186.2 8.2 %collective-permute-start.16 = (f32[10,1,1024]{2,1,0:T(1,128)S(1)}, f32[10,1,1024]{2,1,0:T(1,128)S(1)}, u32[]{:S(2)}, u32[]{:S(2)}) collective-permute-start(f32[10,1,1024]{2,1,0:T(1,128)S(1)} %get-tuple-element.39), channel_id=1, source_target_pairs={{4,0},{8,4},{12,8},{16,12},{20,16},{24,20},{28,24},{5,1},{9,5},{13... | collective-permute-start | bytes 122888 | tf_op jit(solution)/shard_map/ppermute | solution.py:25
  187.5 6.9 %collective-permute-start.17 = (f32[10,1,1024]{2,1,0:T(1,128)S(1)}, f32[10,1,1024]{2,1,0:T(1,128)S(1)}, u32[]{:S(2)}, u32[]{:S(2)}) collective-permute-start(f32[10,1,1024]{2,1,0:T(1,128)S(1)} %get-tuple-element.38), channel_id=1, source_target_pairs={{0,4},{4,8},{8,12},{12,16},{16,20},{20,24},{24,28},{1,5},{5,9},{9,... | collective-permute-start | bytes 122888 | tf_op jit(solution)/shard_map/ppermute | solution.py:23
  196.5 8.0 %collective-permute-start.18 = (f32[10,10,1]{2,1,0:T(8,128)S(1)}, f32[10,10,1]{2,1,0:T(8,128)S(1)}, u32[]{:S(2)}, u32[]{:S(2)}) collective-permute-start(f32[10,10,1]{2,1,0:T(8,128)S(1)} %get-tuple-element.27), channel_id=1, source_target_pairs={{0,1},{1,2},{2,3},{4,5},{5,6},{6,7},{8,9},{9,10},{10,11},{12,13},{... | collective-permute-start | bytes 1208 | tf_op jit(solution)/shard_map/ppermute | solution.py:23
  197.8 6.7 %collective-permute-start.19 = (f32[10,10,1]{2,1,0:T(8,128)S(1)}, f32[10,10,1]{2,1,0:T(8,128)S(1)}, u32[]{:S(2)}, u32[]{:S(2)}) collective-permute-start(f32[10,10,1]{2,1,0:T(8,128)S(1)} %get-tuple-element.26), channel_id=1, source_target_pairs={{1,0},{2,1},{3,2},{5,4},{6,5},{7,6},{9,8},{10,9},{11,10},{13,12},{... | collective-permute-start | bytes 1208 | tf_op jit(solution)/shard_map/ppermute | solution.py:25
  204.5 134.8 %copy-start = (f32[10,8,1024]{2,1,0:T(8,128)S(1)}, f32[10,8,1024]{2,1,0:T(8,128)}, u32[]{:S(2)}) copy-start(f32[10,8,1024]{2,1,0:T(8,128)} %param.21) | copy-start | bytes 983044
  260.9 8.1 %collective-permute-start.20 = (f32[10,1,1024]{2,1,0:T(1,128)S(1)}, f32[10,1,1024]{2,1,0:T(1,128)S(1)}, u32[]{:S(2)}, u32[]{:S(2)}) collective-permute-start(f32[10,1,1024]{2,1,0:T(1,128)S(1)} %get-tuple-element.37), channel_id=1, source_target_pairs={{4,0},{8,4},{12,8},{16,12},{20,16},{24,20},{28,24},{5,1},{9,5},{13... | collective-permute-start | bytes 122888 | tf_op jit(solution)/shard_map/ppermute | solution.py:25
  262.2 6.8 %collective-permute-start.21 = (f32[10,1,1024]{2,1,0:T(1,128)S(1)}, f32[10,1,1024]{2,1,0:T(1,128)S(1)}, u32[]{:S(2)}, u32[]{:S(2)}) collective-permute-start(f32[10,1,1024]{2,1,0:T(1,128)S(1)} %get-tuple-element.36), channel_id=1, source_target_pairs={{0,4},{4,8},{8,12},{12,16},{16,20},{20,24},{24,28},{1,5},{5,9},{9,... | collective-permute-start | bytes 122888 | tf_op jit(solution)/shard_map/ppermute | solution.py:23
  269.0 0.6 copy-start.11
  269.6 0.6 copy-start.12
  270.3 67.1 %all-to-all-start.1 = ((f32[8,8,1024]{2,1,0:T(8,128)}), f32[8,8,1024]{2,1,0:T(8,128)}, u32[]{:S(2)}, u32[]{:S(2)}) async-start(f32[8,8,1024]{2,1,0:T(8,128)} %convolution_bitcast_fusion), calls=%async_computation.1 | async-start | bytes 524288 | tf_op jit(solution)/shard_map/all_to_all | solution.py:145
  276.6 94.7 %all-reduce.12.cloned.1.call-start = ((), (), s32[]{:S(2)}) async-start(), calls=%async_computation.2 | async-start | bytes 262144 | tf_op jit(solution)/shard_map/psum | solution.py:157
  277.4 6.9 %collective-permute-start.22 = (f32[10,10,1]{2,1,0:T(8,128)}, f32[10,10,1]{2,1,0:T(8,128)}, u32[]{:S(2)}, u32[]{:S(2)}) collective-permute-start(f32[10,10,1]{2,1,0:T(8,128)} %get-tuple-element.25), channel_id=1, source_target_pairs={{0,1},{1,2},{2,3},{4,5},{5,6},{6,7},{8,9},{9,10},{10,11},{12,13},{... | collective-permute-start | bytes 1208 | tf_op jit(solution)/shard_map/ppermute | solution.py:23
  279.3 5.4 %collective-permute-start.23 = (f32[10,10,1]{2,1,0:T(8,128)}, f32[10,10,1]{2,1,0:T(8,128)}, u32[]{:S(2)}, u32[]{:S(2)}) collective-permute-start(f32[10,10,1]{2,1,0:T(8,128)} %get-tuple-element.24), channel_id=1, source_target_pairs={{1,0},{2,1},{3,2},{5,4},{6,5},{7,6},{9,8},{10,9},{11,10},{13,12},{... | collective-permute-start | bytes 1208 | tf_op jit(solution)/shard_map/ppermute | solution.py:25
Sparse Core Ops, SparseCore 0:
  339.4 31.8 all-reduce.11
where the time goes:
time: 382 us; the launch traced here: 380 us
  blocking collectives  176 us (46%)
  starting transfers between devices  72.7 us (19%)
  waiting for transfers between devices  42 us (11%)
  other arithmetic  34 us (9%)
  between operations  27.8 us (7%)
  local copies, waits for them, and re-layouts  18.5 us (5%)
  matrix products  8.41 us (2%)
    psum x4, blocking collectives, paired_totals(): lax.psum((jnp.sum(residual * residual), jnp.sum(residual * image)), ('til...  176 us
    ppermute x12, starting transfers between devices, extended(): lax.ppermute(tail, axis, [(i, (i + 1) % count) for i in range(ends)])  44.9 us
    psum x1, waiting for transfers between devices, body(): totals = lax.psum(partial_sums, 'lev')  31.1 us
    ppermute x12, starting transfers between devices, extended(): lax.ppermute(head, axis, [((i + 1) % count, i) for i in range(ends)])  15.7 us
    reduce_sum x4, other arithmetic, paired_totals(): jnp.sum(residual * image)  14 us
  transfers between devices with their start and end apart: 27, of which 7 were waited for; matrix products, arithmetic and copies ran while one was open for 11% of the time, Pallas kernels for 0%

commit v1 on v0

--- a/solution.py
+++ b/solution.py
@@ -154,7 +154,7 @@
         precision=lax.Precision.HIGHEST,
         preferred_element_type=jnp.float32,
     )
-    totals = lax.psum(partial_sums, "lev")
+    totals = jnp.sum(lax.all_gather(partial_sums, "lev"), axis=0)
     ice_smb = totals.reshape(TPD, CX, TW).transpose(1, 0, 2).reshape(CX, TPD * TW)
     ice_frac = ice_mask.astype(jnp.float32)
     rhs = (ice_frac * (thickness + SMB_WEIGHT * prev_smb))[None] * driving

time: 382 us -> 340 us (0.89)
  waiting for transfers between devices: 42 us -> 10.8 us
  between operations: 27.8 us -> 14.7 us
  blocking collectives: 176 us -> 185 us
    psum x1 -> x0, waiting for transfers between devices: 31.1 us -> none  [body(): totals = lax.psum(partial_sums, 'lev')]
    all_gather x0 -> x1, blocking collectives: none -> 8.14 us  [body(): totals = jnp.sum(lax.all_gather(partial_sums, 'lev'), axis=0)]
  transfers between devices with their start and end apart: 27 -> 26, of which waited for: 7 -> 8; matrix products, arithmetic and copies ran while one was open for 11% -> 11% of each run, Pallas kernels for 0% -> 0%
where the time goes in v1:
time: 340 us; the launch traced here: 338 us
  blocking collectives  185 us (54%)
  starting transfers between devices  74.9 us (22%)
  other arithmetic  30.3 us (9%)
  local copies, waits for them, and re-layouts  15.4 us (5%)
  between operations  14.7 us (4%)
  waiting for transfers between devices  10.8 us (3%)
  matrix products  6.9 us (2%)
    psum x4, blocking collectives, paired_totals(): lax.psum((jnp.sum(residual * residual), jnp.sum(residual * image)), ('til...  177 us
    ppermute x12, starting transfers between devices, extended(): lax.ppermute(tail, axis, [(i, (i + 1) % count) for i in range(ends)])  46.3 us
    ppermute x12, starting transfers between devices, extended(): lax.ppermute(head, axis, [((i + 1) % count, i) for i in range(ends)])  15.7 us
    reduce_sum x4, other arithmetic, paired_totals(): jnp.sum(residual * image)  11.4 us
    all_gather x1, blocking collectives, body(): totals = jnp.sum(lax.all_gather(partial_sums, 'lev'), axis=0)  8.14 us
    all_to_all x1, starting transfers between devices, body(): lax.all_to_all(slot_tile, 'tiles', split_axis=0, concat_axis=0, tiled=True)  7.67 us
  transfers between devices with their start and end apart: 26, of which 8 were waited for; matrix products, arithmetic and copies ran while one was open for 11% of the time, Pallas kernels for 0%

profile of v1, /device:TPU:0, one launch (start us, length us, event | category | flops | bytes accessed | tf_op | source)
XLA Modules:
  0.0 338.0 jit_solution(1928182275216769672)
XLA Ops:
  1.8 1.3 collective-permute-start
  3.1 5.5 %collective-permute-start.1 = (f32[10,1,1024]{2,1,0:T(1,128)S(1)}, f32[10,1,1024]{2,1,0:T(1,128)S(1)}, u32[]{:S(2)}, u32[]{:S(2)}) collective-permute-start(f32[10,1,1024]{2,1,0:T(1,128)S(1)} %get-tuple-element.46), channel_id=1, source_target_pairs={{0,4},{4,8},{8,12},{12,16},{16,20},{20,24},{24,28},{1,5},{5,9},{9,... | collective-permute-start | bytes 122888 | tf_op jit(solution)/shard_map/ppermute | solution.py:23
  8.6 1.6 collective-permute-done.1
  11.4 1.3 collective-permute-start.2
  12.7 3.0 collective-permute-start.3
  16.7 2.2 power_multiply_fusion
  18.9 1.3 collective-permute-start.4
  20.2 5.4 %collective-permute-start.5 = (f32[10,1,1024]{2,1,0:T(1,128)S(1)}, f32[10,1,1024]{2,1,0:T(1,128)S(1)}, u32[]{:S(2)}, u32[]{:S(2)}) collective-permute-start(f32[10,1,1024]{2,1,0:T(1,128)S(1)} %get-tuple-element.44), channel_id=1, source_target_pairs={{0,4},{4,8},{8,12},{12,16},{16,20},{20,24},{24,28},{1,5},{5,9},{9,... | collective-permute-start | bytes 122888 | tf_op jit(solution)/shard_map/ppermute | solution.py:23
  25.7 1.4 add_multiply_fusion
  27.6 1.3 collective-permute-start.6
  28.9 3.8 %collective-permute-start.7 = (f32[10,10,1]{2,1,0:T(8,128)S(1)}, f32[10,10,1]{2,1,0:T(8,128)S(1)}, u32[]{:S(2)}, u32[]{:S(2)}) collective-permute-start(f32[10,10,1]{2,1,0:T(8,128)S(1)} %get-tuple-element.32), channel_id=1, source_target_pairs={{0,1},{1,2},{2,3},{4,5},{5,6},{6,7},{8,9},{9,10},{10,11},{12,13},{... | collective-permute-start | bytes 1208 | tf_op jit(solution)/shard_map/ppermute | solution.py:23
  32.6 1.2 fusion.80
  34.7 3.3 fusion.11
  38.1 1.3 collective-permute-start.8
  39.4 5.8 %collective-permute-start.9 = (f32[10,1,1024]{2,1,0:T(1,128)S(1)}, f32[10,1,1024]{2,1,0:T(1,128)S(1)}, u32[]{:S(2)}, u32[]{:S(2)}) collective-permute-start(f32[10,1,1024]{2,1,0:T(1,128)S(1)} %get-tuple-element.42), channel_id=1, source_target_pairs={{0,4},{4,8},{8,12},{12,16},{16,20},{20,24},{24,28},{1,5},{5,9},{9,... | collective-permute-start | bytes 122888 | tf_op jit(solution)/shard_map/ppermute | solution.py:23
  47.0 3.9 %collective-permute-start.10 = (f32[10,10,1]{2,1,0:T(8,128)S(1)}, f32[10,10,1]{2,1,0:T(8,128)S(1)}, u32[]{:S(2)}, u32[]{:S(2)}) collective-permute-start(f32[10,10,1]{2,1,0:T(8,128)S(1)} %get-tuple-element.31), channel_id=1, source_target_pairs={{0,1},{1,2},{2,3},{4,5},{5,6},{6,7},{8,9},{9,10},{10,11},{12,13},{... | collective-permute-start | bytes 1208 | tf_op jit(solution)/shard_map/ppermute | solution.py:23
  50.9 1.3 collective-permute-start.11
  53.5 3.2 collective-permute-done.11
  57.0 1.9 multiply_reduce_fusion.5
  58.9 45.4 %all-reduce.9 = (f32[]{:T(128)}, f32[]{:T(128)}) all-reduce(f32[]{:T(128)} %get-tuple-element.7, f32[]{:T(128)} %get-tuple-element.6), channel_id=1, replica_groups=mesh['tiles'=8,'lev'=4] {'tiles','lev'}, use_global_device_ids=true, to_apply=%region_4.5 | all-reduce | flops 2 | bytes 16 | tf_op jit(solution)/shard_map/psum | solution.py:74
  105.6 1.3 collective-permute-start.12
  106.9 4.8 %collective-permute-start.13 = (f32[10,1,1024]{2,1,0:T(1,128)S(1)}, f32[10,1,1024]{2,1,0:T(1,128)S(1)}, u32[]{:S(2)}, u32[]{:S(2)}) collective-permute-start(f32[10,1,1024]{2,1,0:T(1,128)S(1)} %get-tuple-element.40), channel_id=1, source_target_pairs={{0,4},{4,8},{8,12},{12,16},{16,20},{20,24},{24,28},{1,5},{5,9},{9,... | collective-permute-start | bytes 122888 | tf_op jit(solution)/shard_map/ppermute | solution.py:23
  113.6 1.3 collective-permute-start.14
  114.9 1.3 collective-permute-start.15
  116.9 7.7 %all-to-all-start = ((s32[8,1,8]{2,1,0:T(1,128)}), s32[8,1,8]{2,1,0:T(1,128)}, u32[]{:S(2)}, u32[]{:S(2)}) async-start(s32[8,1,8]{2,1,0:T(1,128)} %bitcast), calls=%async_computation | async-start | bytes 8192 | tf_op jit(solution)/shard_map/all_to_all | solution.py:146
  125.2 1.3 concatenate.135
  126.6 2.9 multiply_reduce_fusion.3
  129.5 44.5 %all-reduce.8 = (f32[]{:T(128)}, f32[]{:T(128)}) all-reduce(f32[]{:T(128)} %get-tuple-element.5, f32[]{:T(128)} %get-tuple-element.4), channel_id=1, replica_groups=mesh['tiles'=8,'lev'=4] {'tiles','lev'}, use_global_device_ids=true, to_apply=%region_8.9 | all-reduce | flops 2 | bytes 16 | tf_op jit(solution)/shard_map/psum | solution.py:74
  178.7 1.3 collective-permute-start.16
  180.0 4.8 %collective-permute-start.17 = (f32[10,1,1024]{2,1,0:T(1,128)S(1)}, f32[10,1,1024]{2,1,0:T(1,128)S(1)}, u32[]{:S(2)}, u32[]{:S(2)}) collective-permute-start(f32[10,1,1024]{2,1,0:T(1,128)S(1)} %get-tuple-element.38), channel_id=1, source_target_pairs={{0,4},{4,8},{8,12},{12,16},{16,20},{20,24},{24,28},{1,5},{5,9},{9,... | collective-permute-start | bytes 122888 | tf_op jit(solution)/shard_map/ppermute | solution.py:23
  187.3 1.3 collective-permute-start.18
  188.6 1.5 collective-permute-start.19
  191.5 3.0 collective-permute-done.19
  195.7 3.3 multiply_reduce_fusion.1
  198.9 42.9 %all-reduce.7 = (f32[]{:T(128)}, f32[]{:T(128)}) all-reduce(f32[]{:T(128)} %get-tuple-element.3, f32[]{:T(128)} %get-tuple-element.2), channel_id=1, replica_groups=mesh['tiles'=8,'lev'=4] {'tiles','lev'}, use_global_device_ids=true, to_apply=%region_12.13 | all-reduce | flops 2 | bytes 16 | tf_op jit(solution)/shard_map/psum | solution.py:74
  245.8 1.7 multiply_reduce_fusion
  247.6 1.3 collective-permute-start.20
  248.9 4.8 %collective-permute-start.21 = (f32[10,1,1024]{2,1,0:T(1,128)S(1)}, f32[10,1,1024]{2,1,0:T(1,128)S(1)}, u32[]{:S(2)}, u32[]{:S(2)}) collective-permute-start(f32[10,1,1024]{2,1,0:T(1,128)S(1)} %get-tuple-element.36), channel_id=1, source_target_pairs={{0,4},{4,8},{8,12},{12,16},{16,20},{20,24},{24,28},{1,5},{5,9},{9,... | collective-permute-start | bytes 122888 | tf_op jit(solution)/shard_map/ppermute | solution.py:23
  253.8 4.6 %fusion.75 = f32[32,1,1024]{2,1,0:T(1,128)S(1)} fusion(bf16[32,128,1024]{2,1,0:T(8,128)(2,1)} %param.12, bf16[32,128,1]{1,0,2:T(8,128)(2,1)S(1)} %bitcast.20), kind=kOutput, calls=%fused_computation.159 | convolution fusion | flops 8388608 | bytes 8527872 | tf_op jit(solution)/shard_map/bl,blt->bt/dot_general | solution.py:124
  260.4 1.9 collective-permute-start.22
  262.3 1.3 collective-permute-start.23
  264.7 5.2 %all-to-all-start.1 = ((f32[8,8,1024]{2,1,0:T(8,128)}), f32[8,8,1024]{2,1,0:T(8,128)}, u32[]{:S(2)}, u32[]{:S(2)}) async-start(f32[8,8,1024]{2,1,0:T(8,128)} %convolution_bitcast_fusion), calls=%async_computation.1 | async-start | bytes 524288 | tf_op jit(solution)/shard_map/all_to_all | solution.py:145
  270.5 2.0 reduce.3
  272.5 1.2 eq.49
  273.7 2.1 concatenate.147
  275.8 3.3 fusion.70
  279.2 44.0 %all-reduce.6 = (f32[]{:T(128)}, f32[]{:T(128)}) all-reduce(f32[]{:T(128)} %get-tuple-element.16, f32[]{:T(128)} %fusion.70), channel_id=1, replica_groups=mesh['tiles'=8,'lev'=4] {'tiles','lev'}, use_global_device_ids=true, to_apply=%region_16.17 | all-reduce | flops 2 | bytes 16 | tf_op jit(solution)/shard_map/psum | solution.py:74
  329.2 8.1 %all-gather = f32[128,1024]{1,0:T(8,128)S(1)} all-gather(f32[32,1024]{1,0:T(8,128)S(1)} %fusion.71), channel_id=2, replica_groups=mesh['tiles'=8,'lev'=4] {'lev'}, dimensions={0}, use_global_device_ids=true | all-gather | bytes 655360 | tf_op jit(solution)/shard_map/all_gather | solution.py:157
  (92 shorter events, 23.0 us)
Async XLA Ops:
  1.8 6.8 %collective-permute-start = (f32[10,1,1024]{2,1,0:T(1,128)S(1)}, f32[10,1,1024]{2,1,0:T(1,128)S(1)}, u32[]{:S(2)}, u32[]{:S(2)}) collective-permute-start(f32[10,1,1024]{2,1,0:T(1,128)S(1)} %get-tuple-element.47), channel_id=1, source_target_pairs={{4,0},{8,4},{12,8},{16,12},{20,16},{24,20},{28,24},{5,1},{9,5},{13... | collective-permute-start | bytes 122888 | tf_op jit(solution)/shard_map/ppermute | solution.py:25
  3.1 7.2 %collective-permute-start.1 = (f32[10,1,1024]{2,1,0:T(1,128)S(1)}, f32[10,1,1024]{2,1,0:T(1,128)S(1)}, u32[]{:S(2)}, u32[]{:S(2)}) collective-permute-start(f32[10,1,1024]{2,1,0:T(1,128)S(1)} %get-tuple-element.46), channel_id=1, source_target_pairs={{0,4},{4,8},{8,12},{12,16},{16,20},{20,24},{24,28},{1,5},{5,9},{9,... | collective-permute-start | bytes 122888 | tf_op jit(solution)/shard_map/ppermute | solution.py:23
  8.6 18.5 %copy-start.6 = (f32[10,1,1024]{2,1,0:T(1,128)}, f32[10,1,1024]{2,1,0:T(1,128)S(1)}, u32[]{:S(2)}) copy-start(f32[10,1,1024]{2,1,0:T(1,128)S(1)} %collective-permute-done) | copy-start | bytes 122884
  10.2 16.9 %copy-start.7 = (f32[10,1,1024]{2,1,0:T(1,128)}, f32[10,1,1024]{2,1,0:T(1,128)S(1)}, u32[]{:S(2)}) copy-start(f32[10,1,1024]{2,1,0:T(1,128)S(1)} %collective-permute-done.1) | copy-start | bytes 122884
  11.4 5.1 %collective-permute-start.2 = (f32[10,10,1]{2,1,0:T(8,128)S(1)}, f32[10,10,1]{2,1,0:T(8,128)S(1)}, u32[]{:S(2)}, u32[]{:S(2)}) collective-permute-start(f32[10,10,1]{2,1,0:T(8,128)S(1)} %get-tuple-element.34), channel_id=1, source_target_pairs={{1,0},{2,1},{3,2},{5,4},{6,5},{7,6},{9,8},{10,9},{11,10},{13,12},{... | collective-permute-start | bytes 1208 | tf_op jit(solution)/shard_map/ppermute | solution.py:25
  12.7 3.9 %collective-permute-start.3 = (f32[10,10,1]{2,1,0:T(8,128)S(1)}, f32[10,10,1]{2,1,0:T(8,128)S(1)}, u32[]{:S(2)}, u32[]{:S(2)}) collective-permute-start(f32[10,10,1]{2,1,0:T(8,128)S(1)} %get-tuple-element.35), channel_id=1, source_target_pairs={{0,1},{1,2},{2,3},{4,5},{5,6},{6,7},{8,9},{9,10},{10,11},{12,13},{... | collective-permute-start | bytes 1208 | tf_op jit(solution)/shard_map/ppermute | solution.py:23
  18.9 8.2 %collective-permute-start.4 = (f32[10,1,1024]{2,1,0:T(1,128)S(1)}, f32[10,1,1024]{2,1,0:T(1,128)S(1)}, u32[]{:S(2)}, u32[]{:S(2)}) collective-permute-start(f32[10,1,1024]{2,1,0:T(1,128)S(1)} %get-tuple-element.45), channel_id=1, source_target_pairs={{4,0},{8,4},{12,8},{16,12},{20,16},{24,20},{28,24},{5,1},{9,5},{13... | collective-permute-start | bytes 122888 | tf_op jit(solution)/shard_map/ppermute | solution.py:25
  20.2 7.1 %collective-permute-start.5 = (f32[10,1,1024]{2,1,0:T(1,128)S(1)}, f32[10,1,1024]{2,1,0:T(1,128)S(1)}, u32[]{:S(2)}, u32[]{:S(2)}) collective-permute-start(f32[10,1,1024]{2,1,0:T(1,128)S(1)} %get-tuple-element.44), channel_id=1, source_target_pairs={{0,4},{4,8},{8,12},{12,16},{16,20},{20,24},{24,28},{1,5},{5,9},{9,... | collective-permute-start | bytes 122888 | tf_op jit(solution)/shard_map/ppermute | solution.py:23
  27.1 86.4 %copy-start.2 = (f32[10,1,1024]{2,1,0:T(1,128)}, f32[10,1,1024]{2,1,0:T(1,128)S(1)}, u32[]{:S(2)}) copy-start(f32[10,1,1024]{2,1,0:T(1,128)S(1)} %collective-permute-done.4) | copy-start | bytes 122884
  27.4 86.2 %copy-start.4 = (f32[10,1,1024]{2,1,0:T(1,128)}, f32[10,1,1024]{2,1,0:T(1,128)S(1)}, u32[]{:S(2)}) copy-start(f32[10,1,1024]{2,1,0:T(1,128)S(1)} %collective-permute-done.5) | copy-start | bytes 122884
  27.6 6.7 %collective-permute-start.6 = (f32[10,10,1]{2,1,0:T(8,128)S(1)}, f32[10,10,1]{2,1,0:T(8,128)S(1)}, u32[]{:S(2)}, u32[]{:S(2)}) collective-permute-start(f32[10,10,1]{2,1,0:T(8,128)S(1)} %get-tuple-element.33), channel_id=1, source_target_pairs={{1,0},{2,1},{3,2},{5,4},{6,5},{7,6},{9,8},{10,9},{11,10},{13,12},{... | collective-permute-start | bytes 1208 | tf_op jit(solution)/shard_map/ppermute | solution.py:25
  28.9 5.4 %collective-permute-start.7 = (f32[10,10,1]{2,1,0:T(8,128)S(1)}, f32[10,10,1]{2,1,0:T(8,128)S(1)}, u32[]{:S(2)}, u32[]{:S(2)}) collective-permute-start(f32[10,10,1]{2,1,0:T(8,128)S(1)} %get-tuple-element.32), channel_id=1, source_target_pairs={{0,1},{1,2},{2,3},{4,5},{5,6},{6,7},{8,9},{9,10},{10,11},{12,13},{... | collective-permute-start | bytes 1208 | tf_op jit(solution)/shard_map/ppermute | solution.py:23
  38.1 8.0 %collective-permute-start.8 = (f32[10,1,1024]{2,1,0:T(1,128)S(1)}, f32[10,1,1024]{2,1,0:T(1,128)S(1)}, u32[]{:S(2)}, u32[]{:S(2)}) collective-permute-start(f32[10,1,1024]{2,1,0:T(1,128)S(1)} %get-tuple-element.43), channel_id=1, source_target_pairs={{4,0},{8,4},{12,8},{16,12},{20,16},{24,20},{28,24},{5,1},{9,5},{13... | collective-permute-start | bytes 122888 | tf_op jit(solution)/shard_map/ppermute | solution.py:25
  39.4 7.4 %collective-permute-start.9 = (f32[10,1,1024]{2,1,0:T(1,128)S(1)}, f32[10,1,1024]{2,1,0:T(1,128)S(1)}, u32[]{:S(2)}, u32[]{:S(2)}) collective-permute-start(f32[10,1,1024]{2,1,0:T(1,128)S(1)} %get-tuple-element.42), channel_id=1, source_target_pairs={{0,4},{4,8},{8,12},{12,16},{16,20},{20,24},{24,28},{1,5},{5,9},{9,... | collective-permute-start | bytes 122888 | tf_op jit(solution)/shard_map/ppermute | solution.py:23
  47.0 6.4 %collective-permute-start.10 = (f32[10,10,1]{2,1,0:T(8,128)S(1)}, f32[10,10,1]{2,1,0:T(8,128)S(1)}, u32[]{:S(2)}, u32[]{:S(2)}) collective-permute-start(f32[10,10,1]{2,1,0:T(8,128)S(1)} %get-tuple-element.31), channel_id=1, source_target_pairs={{0,1},{1,2},{2,3},{4,5},{5,6},{6,7},{8,9},{9,10},{10,11},{12,13},{... | collective-permute-start | bytes 1208 | tf_op jit(solution)/shard_map/ppermute | solution.py:23
  50.9 5.7 %collective-permute-start.11 = (f32[10,10,1]{2,1,0:T(8,128)S(1)}, f32[10,10,1]{2,1,0:T(8,128)S(1)}, u32[]{:S(2)}, u32[]{:S(2)}) collective-permute-start(f32[10,10,1]{2,1,0:T(8,128)S(1)} %get-tuple-element.30), channel_id=1, source_target_pairs={{1,0},{2,1},{3,2},{5,4},{6,5},{7,6},{9,8},{10,9},{11,10},{13,12},{... | collective-permute-start | bytes 1208 | tf_op jit(solution)/shard_map/ppermute | solution.py:25
  105.6 6.9 %collective-permute-start.12 = (f32[10,1,1024]{2,1,0:T(1,128)S(1)}, f32[10,1,1024]{2,1,0:T(1,128)S(1)}, u32[]{:S(2)}, u32[]{:S(2)}) collective-permute-start(f32[10,1,1024]{2,1,0:T(1,128)S(1)} %get-tuple-element.41), channel_id=1, source_target_pairs={{4,0},{8,4},{12,8},{16,12},{20,16},{24,20},{28,24},{5,1},{9,5},{13... | collective-permute-start | bytes 122888 | tf_op jit(solution)/shard_map/ppermute | solution.py:25
  106.9 6.5 %collective-permute-start.13 = (f32[10,1,1024]{2,1,0:T(1,128)S(1)}, f32[10,1,1024]{2,1,0:T(1,128)S(1)}, u32[]{:S(2)}, u32[]{:S(2)}) collective-permute-start(f32[10,1,1024]{2,1,0:T(1,128)S(1)} %get-tuple-element.40), channel_id=1, source_target_pairs={{0,4},{4,8},{8,12},{12,16},{16,20},{20,24},{24,28},{1,5},{5,9},{9,... | collective-permute-start | bytes 122888 | tf_op jit(solution)/shard_map/ppermute | solution.py:23
  112.5 12.1 %copy-start.11 = (f32[10,1,1024]{2,1,0:T(1,128)}, f32[10,1,1024]{2,1,0:T(1,128)S(1)}, u32[]{:S(2)}) copy-start(f32[10,1,1024]{2,1,0:T(1,128)S(1)} %collective-permute-done.12) | copy-start | bytes 122884
  113.4 11.2 %copy-start.12 = (f32[10,1,1024]{2,1,0:T(1,128)}, f32[10,1,1024]{2,1,0:T(1,128)S(1)}, u32[]{:S(2)}) copy-start(f32[10,1,1024]{2,1,0:T(1,128)S(1)} %collective-permute-done.13) | copy-start | bytes 122884
  113.6 11.0 %collective-permute-start.14 = (f32[10,10,1]{2,1,0:T(8,128)S(1)}, f32[10,10,1]{2,1,0:T(8,128)S(1)}, u32[]{:S(2)}, u32[]{:S(2)}) collective-permute-start(f32[10,10,1]{2,1,0:T(8,128)S(1)} %get-tuple-element.29), channel_id=1, source_target_pairs={{0,1},{1,2},{2,3},{4,5},{5,6},{6,7},{8,9},{9,10},{10,11},{12,13},{... | collective-permute-start | bytes 1208 | tf_op jit(solution)/shard_map/ppermute | solution.py:23
  114.9 10.3 %collective-permute-start.15 = (f32[10,10,1]{2,1,0:T(8,128)S(1)}, f32[10,10,1]{2,1,0:T(8,128)}, u32[]{:S(2)}, u32[]{:S(2)}) collective-permute-start(f32[10,10,1]{2,1,0:T(8,128)S(1)} %get-tuple-element.28), channel_id=1, source_target_pairs={{1,0},{2,1},{3,2},{5,4},{6,5},{7,6},{9,8},{10,9},{11,10},{13,12},{... | collective-permute-start | bytes 1208 | tf_op jit(solution)/shard_map/ppermute | solution.py:25
  116.9 147.8 %all-to-all-start = ((s32[8,1,8]{2,1,0:T(1,128)}), s32[8,1,8]{2,1,0:T(1,128)}, u32[]{:S(2)}, u32[]{:S(2)}) async-start(s32[8,1,8]{2,1,0:T(1,128)} %bitcast), calls=%async_computation | async-start | bytes 8192 | tf_op jit(solution)/shard_map/all_to_all | solution.py:146
  124.6 0.6 copy-start.8
  129.5 56.0 %copy-start.1 = (f32[10,8,1024]{2,1,0:T(8,128)}, f32[10,8,1024]{2,1,0:T(8,128)S(1)}, u32[]{:S(2)}) copy-start(f32[10,8,1024]{2,1,0:T(8,128)S(1)} %get-tuple-element.19) | copy-start | bytes 983044
  178.7 6.8 %collective-permute-start.16 = (f32[10,1,1024]{2,1,0:T(1,128)S(1)}, f32[10,1,1024]{2,1,0:T(1,128)S(1)}, u32[]{:S(2)}, u32[]{:S(2)}) collective-permute-start(f32[10,1,1024]{2,1,0:T(1,128)S(1)} %get-tuple-element.39), channel_id=1, source_target_pairs={{4,0},{8,4},{12,8},{16,12},{20,16},{24,20},{28,24},{5,1},{9,5},{13... | collective-permute-start | bytes 122888 | tf_op jit(solution)/shard_map/ppermute | solution.py:25
  180.0 6.5 %collective-permute-start.17 = (f32[10,1,1024]{2,1,0:T(1,128)S(1)}, f32[10,1,1024]{2,1,0:T(1,128)S(1)}, u32[]{:S(2)}, u32[]{:S(2)}) collective-permute-start(f32[10,1,1024]{2,1,0:T(1,128)S(1)} %get-tuple-element.38), channel_id=1, source_target_pairs={{0,4},{4,8},{8,12},{12,16},{16,20},{20,24},{24,28},{1,5},{5,9},{9,... | collective-permute-start | bytes 122888 | tf_op jit(solution)/shard_map/ppermute | solution.py:23
  187.3 4.2 %collective-permute-start.18 = (f32[10,10,1]{2,1,0:T(8,128)}, f32[10,10,1]{2,1,0:T(8,128)S(1)}, u32[]{:S(2)}, u32[]{:S(2)}) collective-permute-start(f32[10,10,1]{2,1,0:T(8,128)} %get-tuple-element.27), channel_id=1, source_target_pairs={{0,1},{1,2},{2,3},{4,5},{5,6},{6,7},{8,9},{9,10},{10,11},{12,13},{... | collective-permute-start | bytes 1208 | tf_op jit(solution)/shard_map/ppermute | solution.py:23
  188.6 5.9 %collective-permute-start.19 = (f32[10,10,1]{2,1,0:T(8,128)}, f32[10,10,1]{2,1,0:T(8,128)S(1)}, u32[]{:S(2)}, u32[]{:S(2)}) collective-permute-start(f32[10,10,1]{2,1,0:T(8,128)} %get-tuple-element.26), channel_id=1, source_target_pairs={{1,0},{2,1},{3,2},{5,4},{6,5},{7,6},{9,8},{10,9},{11,10},{13,12},{... | collective-permute-start | bytes 1208 | tf_op jit(solution)/shard_map/ppermute | solution.py:25
  247.6 10.8 %collective-permute-start.20 = (f32[10,1,1024]{2,1,0:T(1,128)S(1)}, f32[10,1,1024]{2,1,0:T(1,128)S(1)}, u32[]{:S(2)}, u32[]{:S(2)}) collective-permute-start(f32[10,1,1024]{2,1,0:T(1,128)S(1)} %get-tuple-element.37), channel_id=1, source_target_pairs={{4,0},{8,4},{12,8},{16,12},{20,16},{24,20},{28,24},{5,1},{9,5},{13... | collective-permute-start | bytes 122888 | tf_op jit(solution)/shard_map/ppermute | solution.py:25
  248.9 9.5 %collective-permute-start.21 = (f32[10,1,1024]{2,1,0:T(1,128)S(1)}, f32[10,1,1024]{2,1,0:T(1,128)S(1)}, u32[]{:S(2)}, u32[]{:S(2)}) collective-permute-start(f32[10,1,1024]{2,1,0:T(1,128)S(1)} %get-tuple-element.36), channel_id=1, source_target_pairs={{0,4},{4,8},{8,12},{12,16},{16,20},{20,24},{24,28},{1,5},{5,9},{9,... | collective-permute-start | bytes 122888 | tf_op jit(solution)/shard_map/ppermute | solution.py:23
  253.7 9.8 %copy-start.13 = (s32[32]{0:T(128)S(1)}, s32[32]{0:T(128)}, u32[]{:S(2)}) copy-start(s32[32]{0:T(128)} %multiply_add_fusion.2) | copy-start | bytes 388
  253.7 22.1 %copy-start.3 = (f32[10,1,1024]{2,1,0:T(1,128)S(1)}, f32[10,1,1024]{2,1,0:T(1,128)}, u32[]{:S(2)}) copy-start(f32[10,1,1024]{2,1,0:T(1,128)} %copy-done.2) | copy-start | bytes 122884
  253.8 22.1 %copy-start.5 = (f32[10,1,1024]{2,1,0:T(1,128)S(1)}, f32[10,1,1024]{2,1,0:T(1,128)}, u32[]{:S(2)}) copy-start(f32[10,1,1024]{2,1,0:T(1,128)} %copy-done.4) | copy-start | bytes 122884
  253.8 73.3 %copy-start = (f32[10,8,1024]{2,1,0:T(8,128)S(1)}, f32[10,8,1024]{2,1,0:T(8,128)}, u32[]{:S(2)}) copy-start(f32[10,8,1024]{2,1,0:T(8,128)} %param.21) | copy-start | bytes 983044
  258.4 0.6 copy-start.9
  259.0 0.6 copy-start.10
  260.4 13.3 %collective-permute-start.22 = (f32[10,10,1]{2,1,0:T(8,128)}, f32[10,10,1]{2,1,0:T(8,128)}, u32[]{:S(2)}, u32[]{:S(2)}) collective-permute-start(f32[10,10,1]{2,1,0:T(8,128)} %get-tuple-element.25), channel_id=1, source_target_pairs={{0,1},{1,2},{2,3},{4,5},{5,6},{6,7},{8,9},{9,10},{10,11},{12,13},{... | collective-permute-start | bytes 1208 | tf_op jit(solution)/shard_map/ppermute | solution.py:23
  262.3 11.4 %collective-permute-start.23 = (f32[10,10,1]{2,1,0:T(8,128)}, f32[10,10,1]{2,1,0:T(8,128)}, u32[]{:S(2)}, u32[]{:S(2)}) collective-permute-start(f32[10,10,1]{2,1,0:T(8,128)} %get-tuple-element.24), channel_id=1, source_target_pairs={{1,0},{2,1},{3,2},{5,4},{6,5},{7,6},{9,8},{10,9},{11,10},{13,12},{... | collective-permute-start | bytes 1208 | tf_op jit(solution)/shard_map/ppermute | solution.py:25
  264.7 63.3 %all-to-all-start.1 = ((f32[8,8,1024]{2,1,0:T(8,128)}), f32[8,8,1024]{2,1,0:T(8,128)}, u32[]{:S(2)}, u32[]{:S(2)}) async-start(f32[8,8,1024]{2,1,0:T(8,128)} %convolution_bitcast_fusion), calls=%async_computation.1 | async-start | bytes 524288 | tf_op jit(solution)/shard_map/all_to_all | solution.py:145
